TPU v7x, 256 devices: a whole 4x4x8 slice. The times are simulated.
256 devices in a mesh: dp: 16 (over z, y_lo), tensor: 4 (over x), section: 4 (over y_hi, core).
Axes of the slice: x: 4, y: 4 (y_hi: 2, y_lo: 2; y = y_hi * 2 + y_lo), z: 8, core: 2. Of those that a mesh axis runs over, the one named last changes fastest.
Arguments:
- grad_parts: bfloat16 [4, 16, 4, 1024, 1024], P('section', 'dp', None, None, 'tensor'), may hold values from -1.5 to 1.5
- first_moment: float32 [4, 4, 1024, 1024], P('section', 'tensor', 'dp'), may hold values from -3 to 3
- second_moment: float32 [4, 4, 1024, 1024], P('section', 'tensor', 'dp'), may hold values from 0.1 to 4
- left_stat: float32 [4, 4, 1024, 1024], P('section', 'tensor', 'dp'), may hold values from -12288 to 184320
- right_stat: float32 [4, 4, 1024, 1024], P('section', 'tensor', 'dp'), may hold values from -12288 to 184320
- left_basis: float32 [4, 4, 1024, 1024], P('section', 'tensor', 'dp'), may hold values from -0.1875 to 0.1875
- right_basis: float32 [4, 4, 1024, 1024], P('section', 'tensor', 'dp'), may hold values from -0.1875 to 0.1875
- gain_grads: float32 [4, 16, 4, 2, 1024], P('section', 'dp', 'tensor'), may hold values from -1.2 to 1.2
- gain_first: float32 [4, 2, 1024], P('section'), may hold values from -3 to 3
- gain_second: float32 [4, 2, 1024], P('section'), may hold values from 0.1 to 4
- table_grads: float32 [4, 16, 32, 16], P('section', 'dp', None, 'tensor'), may hold values from -1.2 to 1.2
- table_first: float32 [32, 16], P(None, 'tensor'), may hold values from -3 to 3
- table_second: float32 [32, 16], P(None, 'tensor'), may hold values from 0.1 to 4
Outputs:
- update: float32 [4, 4, 1024, 1024], P('section', 'tensor', 'dp')
- first_next: float32 [4, 4, 1024, 1024], P('section', 'tensor', 'dp')
- second_next: float32 [4, 4, 1024, 1024], P('section', 'tensor', 'dp')
- left_next: float32 [4, 4, 1024, 1024], P('section', 'tensor', 'dp')
- right_next: float32 [4, 4, 1024, 1024], P('section', 'tensor', 'dp')
- left_rotation: float32 [4, 4, 1024, 1024], P('section', 'tensor', 'dp')
- right_rotation: float32 [4, 4, 1024, 1024], P('section', 'tensor', 'dp')
- gain_update: float32 [4, 2, 1024], P('section')
- gain_moment: float32 [4, 2, 1024], P('section')
- gain_squares: float32 [4, 2, 1024], P('section')
- table_update: float32 [32, 16], P(None, 'tensor')
- table_moment: float32 [32, 16], P(None, 'tensor')
- table_squares: float32 [32, 16], P(None, 'tensor')
All inputs are finite; a program needn't handle non-finite values.
Results may differ from a plain program's by a relative error of at most 0.014.
Values may be sent and summed in bfloat16 or wider, within the bound.
A program may use at most 64 MiB of HBM per device.

v0:
```python
import jax
import jax.numpy as jnp
from jax import lax
from jax.sharding import PartitionSpec as P

NS_ITERS = 3


beta_first = 0.9
beta_second = 0.95
beta_stat = 0.95
adam_eps = 1e-08
norm_eps = 1e-06
step_count = 10.0


def to_half(value):
    return value.astype(jnp.bfloat16)


def batched(pattern, left, right):
    return jnp.einsum(pattern, left, right, preferred_element_type=jnp.float32)


def adam_direction(first, second):
    first_hat = first / (1.0 - beta_first**step_count)
    second_hat = second / (1.0 - beta_second**step_count)
    return first_hat / (jnp.sqrt(second_hat) + adam_eps)


def local(
    grad_parts,
    first_moment,
    second_moment,
    left_stat,
    right_stat,
    left_basis,
    right_basis,
    gain_grads,
    gain_first,
    gain_second,
    table_grads,
    table_first,
    table_second,
):
    partial_value = grad_parts[0, 0]
    columns = lax.all_to_all(partial_value, "tensor", split_axis=0, concat_axis=2, tiled=True)
    summed = lax.psum_scatter(
        columns.astype(jnp.float32).astype(jnp.bfloat16), "dp", scatter_dimension=1, tiled=True
    ).astype(jnp.float32)
    grad_rows = to_half(summed)
    row_count = grad_rows.shape[1]
    offset = lax.axis_index("dp") * row_count
    left_local = to_half(left_basis[0])
    right_local = to_half(right_basis[0])
    left_full, right_full = (
        lax.all_gather(left_local, "dp", axis=1, tiled=True),
        lax.all_gather(right_local, "dp", axis=1, tiled=True),
    )
    grad_full = lax.all_gather(grad_rows, "dp", axis=1, tiled=True)
    rotated_half = to_half(batched("mik,mkj->mij", grad_rows, right_full))
    block = left_local
    rotated = jnp.swapaxes(
        lax.psum_scatter(
            batched("mkc,mkj->cmj", block, rotated_half), "dp", scatter_dimension=0, tiled=True
        ),
        0,
        1,
    )
    first_new = beta_first * first_moment[0] + (1.0 - beta_first) * rotated
    second_new = beta_second * second_moment[0] + (1.0 - beta_second) * rotated * rotated
    direction = to_half(adam_direction(first_new, second_new))
    block = left_local
    back_half = to_half(
        batched("mik,mkj->mij", block, lax.all_gather(direction, "dp", axis=1, tiled=True))
    )
    update = batched("mik,mjk->mij", back_half, right_full)
    grad_columns = lax.dynamic_slice_in_dim(grad_full, offset, row_count, 2)
    left_new = beta_stat * left_stat[0] + batched("mik,mjk->mij", grad_rows, grad_full)
    right_new = beta_stat * right_stat[0] + batched("mki,mkj->mij", grad_columns, grad_full)
    power_left = batched("mik,mkj->mij", to_half(left_new), left_full)
    power_right = batched("mik,mkj->mij", to_half(right_new), right_full)
    power = jnp.concatenate([power_left, power_right], axis=0)
    squares = lax.psum(jnp.sum(power * power, axis=(1, 2)), "dp")
    iterate = power / jnp.sqrt(squares + norm_eps)[:, None, None]
    for sweep in range(NS_ITERS):
        iterate_half = to_half(iterate)
        iterate_full = lax.all_gather(iterate_half, "dp", axis=1, tiled=True)
        gram = to_half(batched("mik,mjk->mij", iterate_half, iterate_full))
        iterate = 1.5 * iterate - 0.5 * batched("mik,mkj->mij", gram, iterate_full)
    local_mats = power_left.shape[0]
    left_rotation = iterate[:local_mats]
    right_rotation = iterate[local_mats:]
    gain_sum = lax.psum(gain_grads[0, 0, 0], ("dp", "tensor"))
    gain_moment = beta_first * gain_first[0] + (1.0 - beta_first) * gain_sum
    gain_squares = beta_second * gain_second[0] + (1.0 - beta_second) * gain_sum * gain_sum
    gain_update = adam_direction(gain_moment, gain_squares)
    table_sum = lax.psum(table_grads[0, 0], ("dp", "section"))
    table_moment = beta_first * table_first + (1.0 - beta_first) * table_sum
    table_squares = beta_second * table_second + (1.0 - beta_second) * table_sum * table_sum
    table_update = adam_direction(table_moment, table_squares)
    return (
        update[None],
        first_new[None],
        second_new[None],
        left_new[None],
        right_new[None],
        left_rotation[None],
        right_rotation[None],
        gain_update[None],
        gain_moment[None],
        gain_squares[None],
        table_update,
        table_moment,
        table_squares,
    )


def solution(mesh):
    return jax.shard_map(
        local,
        mesh=mesh,
        in_specs=(
            P("section", "dp", None, None, "tensor"),
            P("section", "tensor", "dp", None),
            P("section", "tensor", "dp", None),
            P("section", "tensor", "dp", None),
            P("section", "tensor", "dp", None),
            P("section", "tensor", "dp", None),
            P("section", "tensor", "dp", None),
            P("section", "dp", "tensor", None, None),
            P("section", None, None),
            P("section", None, None),
            P("section", "dp", None, "tensor"),
            P(None, "tensor"),
            P(None, "tensor"),
        ),
        out_specs=(
            P("section", "tensor", "dp", None),
            P("section", "tensor", "dp", None),
            P("section", "tensor", "dp", None),
            P("section", "tensor", "dp", None),
            P("section", "tensor", "dp", None),
            P("section", "tensor", "dp", None),
            P("section", "tensor", "dp", None),
            P("section", None, None),
            P("section", None, None),
            P("section", None, None),
            P(None, "tensor"),
            P(None, "tensor"),
            P(None, "tensor"),
        ),
        check_vma=False,
    )
```

profile of v0, /device:TPU:2, one launch (start us, length us, event | category | flops | bytes accessed | tf_op | source)
XLA Modules:
  0.0 1098.2 jit_solution(950655685034763806)
XLA Ops:
  7.2 4.0 copy.47
  11.2 29.7 %all_to_all.18 = bf16[4,1024,256]{1,2,0:T(8,128)(2,1)S(1)} all-to-all(bf16[4,1024,256]{1,2,0:T(8,128)(2,1)} %bitcast.140), channel_id=1, replica_groups=mesh['dp'=16,'tensor'=4,'section'=4] {'tensor'}, dimensions={0} | all-to-all | bytes 4194304 | tf_op jit(solution)/shard_map/all_to_all | solution.py:47
  40.9 7.8 copy.50
  48.7 4.4 copy.60
  53.1 77.8 %reduce-scatter.4.cloned.1.call-done = bf16[64,1024]{1,0:T(8,128)(2,1)} async-done(((bf16[1024,1024]{1,0:T(8,128)(2,1)}), bf16[64,1024]{1,0:T(8,128)(2,1)}) %reduce-scatter.4.cloned.1.call-update) | async-done | bytes 131088
  134.5 70.3 %all-gather.12.cloned.1.call-done = bf16[1,1024,1024]{2,1,0:T(8,128)(2,1)} async-done(((bf16[1,64,1024]{2,1,0:T(8,128)(2,1)}), bf16[1,1024,1024]{2,1,0:T(8,128)(2,1)}) %all-gather.12.cloned.1.call-update) | async-done | bytes 2097168 | tf_op jit(solution)/shard_map/all_gather | solution.py:60
  204.7 2.5 fusion.20
  207.2 70.5 %all-gather.20.cloned.1.call-done = bf16[1,1,1024,1024]{3,2,1,0:T(8,128)(2,1)} async-done(((bf16[1,1,64,1024]{3,2,1,0:T(8,128)(2,1)}), bf16[1,1,1024,1024]{3,2,1,0:T(8,128)(2,1)}) %all-gather.20.cloned.1.call-update) | async-done | bytes 2097168 | tf_op jit(solution)/shard_map/all_gather | solution.py:58
  277.7 2.1 fusion.26
  280.6 69.9 %all-gather.22.cloned.1.call-done = bf16[1,1,1024,1024]{3,2,1,0:T(8,128)(2,1)} async-done(((bf16[1,1,64,1024]{3,2,1,0:T(8,128)(2,1)}), bf16[1,1,1024,1024]{3,2,1,0:T(8,128)(2,1)}) %all-gather.22.cloned.1.call-update) | async-done | bytes 2097168 | tf_op jit(solution)/shard_map/all_gather | solution.py:57
  350.5 2.1 fusion.29
  352.8 32.8 %psum.21 = f32[2]{0:T(128)S(1)} all-reduce(f32[2]{0:T(128)S(1)} %multiply_reduce_fusion), channel_id=1, replica_groups=mesh['dp'=16,'tensor'=4,'section'=4] {'dp'}, use_global_device_ids=true, to_apply=%region_3.0 | all-reduce | flops 2 | bytes 16 | tf_op jit(solution)/shard_map/psum | solution.py:84
  386.5 3.2 convolution_bitcast_fusion
  389.7 11.0 %copy.48 = f32[1024,1,1024]{2,1,0:T(1,128)} copy(f32[1024,1,1024]{0,2,1:T(8,128)} %convolution_bitcast_fusion) | data formatting | bytes 8388608 | tf_op jit(solution)/shard_map/mkc,mkj->cmj/transpose | solution.py:22
  400.9 84.0 %all-gather.14.cloned.1.call-done = bf16[2,1024,1024]{2,1,0:T(8,128)(2,1)} async-done(((bf16[2,64,1024]{2,1,0:T(8,128)(2,1)}), bf16[2,1024,1024]{2,1,0:T(8,128)(2,1)}) %all-gather.14.cloned.1.call-update) | async-done | bytes 4194320 | tf_op jit(solution)/shard_map/all_gather | solution.py:88
  484.9 6.5 fusion.73
  492.7 193.9 %all-reduce.3.cloned.1.call-done = f32[1024,1,1024]{2,1,0:T(1,128)} async-done(((f32[1024,1,1024]{2,1,0:T(1,128)}), f32[1024,1,1024]{2,1,0:T(1,128)}) %all-reduce.3.cloned.1.call-update) | async-done | bytes 4194320
  688.5 99.6 %all-gather.16.cloned.1.call-done = bf16[2,1024,1024]{2,1,0:T(8,128)(2,1)} async-done(((bf16[2,64,1024]{2,1,0:T(8,128)(2,1)}), bf16[2,1024,1024]{2,1,0:T(8,128)(2,1)}) %all-gather.16.cloned.1.call-update) | async-done | bytes 4194320 | tf_op jit(solution)/shard_map/all_gather | solution.py:88
  788.1 6.4 fusion.76
  794.6 128.0 %psum.23 = f32[32,4]{0,1:T(4,128)} all-reduce(f32[32,4]{0,1:T(4,128)S(1)} %bitcast.144), channel_id=1, replica_groups=mesh['dp'=16,'tensor'=4,'section'=4] {'dp','section'}, use_global_device_ids=true, to_apply=%region_5.0 | all-reduce | flops 128 | bytes 1024 | tf_op jit(solution)/shard_map/psum | solution.py:98
  922.6 155.6 %psum.22 = f32[2,1024]{1,0:T(2,128)S(1)} all-reduce(f32[2,1024]{1,0:T(2,128)S(1)} %bitcast.143), channel_id=1, replica_groups=mesh['dp'=16,'tensor'=4,'section'=4] {'dp','tensor'}, use_global_device_ids=true, to_apply=%region_4.0 | all-reduce | flops 2048 | bytes 16384 | tf_op jit(solution)/shard_map/psum | solution.py:94
  1079.5 1.4 fusion.69
  1081.8 3.5 fusion.23
  1085.3 5.6 fusion.14
  (65 shorter events, 11.1 us)
Async XLA Ops:
  7.2 123.7 %reduce-scatter.4.cloned.1.call-start = ((), (), s32[]{:S(2)}) async-start(), calls=%async_computation.9 | async-start | bytes 2228224
  53.0 79.7 %copy-start.8 = (f32[1,1,64,1024]{3,2,1,0:T(8,128)S(1)}, f32[1,1,64,1024]{3,2,1,0:T(8,128)}, u32[]{:S(2)}) copy-start(f32[1,1,64,1024]{3,2,1,0:T(8,128)} %param.19) | copy-start | bytes 786436
  53.0 80.5 %copy-start.9 = (f32[1,1,64,1024]{3,2,1,0:T(8,128)S(1)}, f32[1,1,64,1024]{3,2,1,0:T(8,128)}, u32[]{:S(2)}) copy-start(f32[1,1,64,1024]{3,2,1,0:T(8,128)} %param.18) | copy-start | bytes 786436
  53.0 151.7 %copy-start.10 = (f32[1,1,64,1024]{3,2,1,0:T(8,128)S(1)}, f32[1,1,64,1024]{3,2,1,0:T(8,128)}, u32[]{:S(2)}) copy-start(f32[1,1,64,1024]{3,2,1,0:T(8,128)} %param.17) | copy-start | bytes 786436
  53.1 151.7 %all-gather.12.cloned.1.call-start = ((), (), s32[]{:S(2)}) async-start(), calls=%async_computation.3 | async-start | bytes 2228224 | tf_op jit(solution)/shard_map/all_gather | solution.py:60
  132.7 145.0 %all-gather.20.cloned.1.call-start = ((), (), s32[]{:S(2)}) async-start(), calls=%async_computation.7 | async-start | bytes 2228224 | tf_op jit(solution)/shard_map/all_gather | solution.py:58
  133.5 217.1 %all-gather.22.cloned.1.call-start = ((), (), s32[]{:S(2)}) async-start(), calls=%async_computation.8 | async-start | bytes 2228224 | tf_op jit(solution)/shard_map/all_gather | solution.py:57
  134.2 350.7 %all-gather.14.cloned.1.call-start = ((), (), s32[]{:S(2)}) async-start(), calls=%async_computation.4 | async-start | bytes 4456448 | tf_op jit(solution)/shard_map/all_gather | solution.py:88
  134.5 145.3 %copy-start.11 = (f32[1,1,64,1024]{3,2,1,0:T(8,128)S(1)}, f32[1,1,64,1024]{3,2,1,0:T(8,128)}, u32[]{:S(2)}) copy-start(f32[1,1,64,1024]{3,2,1,0:T(8,128)} %param.16) | copy-start | bytes 786436
  204.7 75.0 %copy-start.1 = (bf16[1,1024,1024]{2,1,0:T(8,128)(2,1)S(1)}, bf16[1,1024,1024]{2,1,0:T(8,128)(2,1)}, u32[]{:S(2)}) copy-start(bf16[1,1024,1024]{2,1,0:T(8,128)(2,1)} %all-gather.12.cloned.1.call-done) | copy-start | bytes 6291460
  207.2 73.4 %copy-start.6 = (f32[64,1024]{1,0:T(8,128)}, f32[64,1024]{1,0:T(8,128)S(1)}, u32[]{:S(2)}) copy-start(f32[64,1024]{1,0:T(8,128)S(1)} %fusion.20) | copy-start | bytes 786436
  280.6 105.9 %copy-start.7 = (f32[64,1024]{1,0:T(8,128)}, f32[64,1024]{1,0:T(8,128)S(1)}, u32[]{:S(2)}) copy-start(f32[64,1024]{1,0:T(8,128)S(1)} %fusion.17) | copy-start | bytes 786436
  280.6 105.9 %copy-start = (bf16[1,1,1024,1024]{3,2,1,0:T(8,128)(2,1)S(1)}, bf16[1,1,1024,1024]{3,2,1,0:T(8,128)(2,1)}, u32[]{:S(2)}) copy-start(bf16[1,1,1024,1024]{3,2,1,0:T(8,128)(2,1)} %all-gather.20.cloned.1.call-done) | copy-start | bytes 6291460
  280.6 105.9 %copy-start.3 = (bf16[1,1,64,1024]{3,2,1,0:T(8,128)(2,1)S(1)}, bf16[1,1,64,1024]{3,2,1,0:T(8,128)(2,1)}, u32[]{:S(2)}) copy-start(bf16[1,1,64,1024]{3,2,1,0:T(8,128)(2,1)} %convert_element_type.87) | copy-start | bytes 393220
  386.4 300.2 %all-reduce.3.cloned.1.call-start = ((), (), s32[]{:S(2)}) async-start(), calls=%async_computation.10 | async-start | bytes 8388608
  400.8 90.7 %copy-start.14 = (u32[256]{0:T(256)S(1)}, u32[256]{0:T(256)}, u32[]{:S(2)}) copy-start(u32[256]{0:T(256)} %constant.66) | copy-start | bytes 3076
  400.8 286.8 %copy-start.4 = (f32[1,1,64,1024]{3,2,1,0:T(8,128)S(1)}, f32[1,1,64,1024]{3,2,1,0:T(8,128)}, u32[]{:S(2)}) copy-start(f32[1,1,64,1024]{3,2,1,0:T(8,128)} %param.15) | copy-start | bytes 786436
  400.8 286.8 %copy-start.5 = (f32[1,1,64,1024]{3,2,1,0:T(8,128)S(1)}, f32[1,1,64,1024]{3,2,1,0:T(8,128)}, u32[]{:S(2)}) copy-start(f32[1,1,64,1024]{3,2,1,0:T(8,128)} %param.14) | copy-start | bytes 786436
  400.8 387.3 %all-gather.16.cloned.1.call-start = ((), (), s32[]{:S(2)}) async-start(), calls=%async_computation.5 | async-start | bytes 4456448 | tf_op jit(solution)/shard_map/all_gather | solution.py:88
  491.4 590.4 %all-gather.10.cloned.1.call-start = ((), (), s32[]{:S(2)}) async-start(), calls=%async_computation.2 | async-start | bytes 2228224 | tf_op jit(solution)/shard_map/all_gather | solution.py:75
  688.5 396.8 %all-gather.18.cloned.1.call-start = ((), (), s32[]{:S(2)}) async-start(), calls=%async_computation.6 | async-start | bytes 4456448 | tf_op jit(solution)/shard_map/all_gather | solution.py:88
  788.1 6.5 copy-start.13
  788.1 134.5 %copy-start.12 = (f32[1,1,1,2,1024]{4,3,2,1,0:T(2,128)S(1)}, f32[1,1,1,2,1024]{4,3,2,1,0:T(2,128)}, u32[]{:S(2)}) copy-start(f32[1,1,1,2,1024]{4,3,2,1,0:T(2,128)} %param.20) | copy-start | bytes 24580
  1081.8 3.5 copy-start.2
Sparse Core Ops, SparseCore 0:
  53.2 77.7 reduce-scatter.3
  133.3 71.4 all-gather.11
  207.1 70.5 all-gather.19
  279.9 70.5 all-gather.21
  386.5 98.3 all-gather.13
  487.4 199.1 all-reduce.2
  689.0 99.1 all-gather.15
  790.5 73.1 all-gather.9
  866.1 98.3 all-gather.17
where the time goes:
time: 1100 us
  waiting for transfers between devices  666 us (61%)
  blocking collectives  346 us (31%)
  matrix products  32.5 us (3%)
  local copies, waits for them, and re-layouts  31.6 us (3%)
  between operations  14.7 us (1%)
    unnamed x11, waiting for transfers between devices  272 us
    all_gather x3, waiting for transfers between devices, local(): iterate_full = lax.all_gather(iterate_half, 'dp', axis=1, tiled=True)  184 us
    psum x1, blocking collectives, local(): gain_sum = lax.psum(gain_grads[0, 0, 0], ('dp', 'tensor'))  156 us
    psum x1, blocking collectives, local(): table_sum = lax.psum(table_grads[0, 0], ('dp', 'section'))  128 us
    all_gather x1, waiting for transfers between devices, local(): lax.all_gather(right_local, 'dp', axis=1, tiled=True)  70.5 us
    all_gather x1, waiting for transfers between devices, local(): grad_full = lax.all_gather(grad_rows, 'dp', axis=1, tiled=True)  70.3 us
    all_gather x1, waiting for transfers between devices, local(): lax.all_gather(left_local, 'dp', axis=1, tiled=True)  69.9 us
    psum x1, blocking collectives, local(): squares = lax.psum(jnp.sum(power * power, axis=(1, 2)), 'dp')  32.8 us
  transfers between devices with their start and end apart: 9, of which 7 were waited for; matrix products, arithmetic and copies ran while one was open for 4% of the time, Pallas kernels for 0%

commit v1 on v0

v1 whole, which is shorter than its diff:
```python
import jax
import jax.numpy as jnp
from jax import lax
from jax.experimental import pallas as pl
from jax.experimental.pallas import tpu as pltpu
from jax.sharding import PartitionSpec as P

MESH = pl.DeviceIdType.MESH
F32, BF16 = jnp.float32, jnp.bfloat16

beta_first = 0.9
beta_second = 0.95
beta_stat = 0.95
adam_eps = 1e-08
norm_eps = 1e-06
step_count = 10.0

D = 1024
NZ = 8
BLK = D // NZ
ROWS = BLK // 2
COLS = D // 4
HALF = D // 2
TILE = 256


def adam_direction(first, second):
    first_hat = first / (1.0 - beta_first**step_count)
    second_hat = second / (1.0 - beta_second**step_count)
    return first_hat / (jnp.sqrt(second_hat) + adam_eps)


def dot_nn(a, b):
    return jnp.dot(a, b, preferred_element_type=F32)


def dot_nt(a, b):
    return lax.dot_general(a, b, (((1,), (1,)), ((), ())), preferred_element_type=F32)


def dot_tn(a, b):
    return lax.dot_general(a, b, (((0,), (0,)), ((), ())), preferred_element_type=F32)


def wrap(value, size):
    return lax.rem(value + 2 * size, size)


def kernel(
    g, m1, m2, ls, rs, lb, rb, gg, gf, gs, tg, tf, ts,
    o_update, o_first, o_second, o_left, o_right, o_lrot, o_rrot,
    o_gu, o_gm, o_gs, o_tu, o_tm, o_ts,
    left128, basis_send, basis, grad, xhalf, xa, xb, gram, xf, ehalf,
    rs_recv, rs_send, zsum, ysum, gx, stat_recv, next_half,
    s_buf, rot, rot_send, d128, e_send, upd_send, upd_recv, fin_send, fin_recv,
    gain_x, gain_y, gain_ys, gain_z, tab_s, tab_y, tab_ys, tab_z,
    ring_ss, ring_rs, y_ss, y_rs, x_ss, x_rs, small_ss, small_rs, sring_ss, sring_rs,
):
    dp = lax.axis_index("dp")
    x = lax.axis_index("tensor")
    sec = lax.axis_index("section")
    z = dp // 2
    y = lax.rem(dp, 2)
    up = {"dp": wrap(z + 1, NZ) * 2 + y}
    down = {"dp": wrap(z - 1, NZ) * 2 + y}
    partner = {"dp": z * 2 + 1 - y}
    pending = []

    def remote(src, dst, ssem, rsem, device):
        return pltpu.make_async_remote_copy(
            src_ref=src, dst_ref=dst, send_sem=ssem, recv_sem=rsem,
            device_id=device, device_id_type=MESH,
        )

    def send(*spec):
        copy = remote(*spec)
        copy.start()
        pending.append(copy)

    def xpeer(k):
        return {"tensor": lax.rem(x + k, 4)}

    def speer(k):
        return {"section": lax.rem(sec + k, 4)}

    barrier = pltpu.get_barrier_semaphore()
    peers = [up, down, partner] + [xpeer(k) for k in (1, 2, 3)] + [speer(k) for k in (1, 2, 3)]
    for peer in peers:
        pl.semaphore_signal(barrier, inc=1, device_id=peer, device_id_type=MESH)
    pl.semaphore_wait(barrier, len(peers))

    def rows(block, sub):
        return pl.ds(pl.multiple_of(block * BLK + sub * ROWS, ROWS), ROWS)

    def blk(block):
        return pl.ds(pl.multiple_of(block * BLK, BLK), BLK)

    mine = blk(z)
    own_sub = pl.ds(pl.multiple_of(y * ROWS, ROWS), ROWS)

    def ring_spec(phase, buf, direction, m, at_sender):
        step = m // 2
        swapped = (m % 2 == 1) if m < 6 else (direction == 1)
        sub = (1 - y) if swapped else y
        sign = -1 if direction == 0 else 1
        origin = z if at_sender else z + sign
        block = wrap(origin + sign * step, NZ)
        part = buf.at[rows(block, sub), :]
        device = up if direction == 0 else down
        return (
            part, part, ring_ss.at[phase, direction, m], ring_rs.at[phase, direction, m], device,
        )

    def ring_send(phase, buf, m):
        for direction in (0, 1):
            send(*ring_spec(phase, buf, direction, m, True))

    def ring_wait(phase, buf, m):
        for direction in (0, 1):
            remote(*ring_spec(phase, buf, direction, m, False)).wait_recv()

    def ring_step(phase, buf, m):
        ring_wait(phase, buf, m)
        if m < 4:
            ring_send(phase, buf, m + 2)
        elif m == 4:
            send(*ring_spec(phase, buf, 0, 6, True))
        elif m == 5:
            send(*ring_spec(phase, buf, 1, 6, True))

    def rs_chunk(direction, step):
        return wrap(z - 1 - step if direction == 0 else z + 1 + step, NZ)

    def rs_copy(direction, step, src):
        send(
            src, rs_recv.at[direction, step], ring_ss.at[0, direction, step],
            ring_rs.at[0, direction, step], up if direction == 0 else down,
        )

    for direction in (0, 1):
        rs_copy(direction, 0, g.at[pl.ds(2 * direction, 2), blk(rs_chunk(direction, 0)), :])

    lhalf = lb[...].astype(BF16)
    rhalf = rb[...].astype(BF16)
    left128[own_sub, :] = lhalf

    @pl.when(y == 0)
    def _():
        basis[rows(z, 0), :] = lhalf
        basis_send[...] = rhalf

    @pl.when(y == 1)
    def _():
        basis[rows(z, 1), :] = rhalf
        basis_send[...] = lhalf

    send(basis_send, basis.at[rows(z, y), :], y_ss.at[0], y_rs.at[0], partner)
    ring_send(1, basis, 0)
    send(left128.at[own_sub, :], left128.at[own_sub, :], y_ss.at[1], y_rs.at[1], partner)

    def stat_copy(src):
        return remote(src, stat_recv, y_ss.at[2], y_rs.at[2], partner)

    @pl.when(y == 0)
    def _():
        stat_copy(rs).start()

    @pl.when(y == 1)
    def _():
        stat_copy(ls).start()

    pending.append(stat_copy(ls))

    for k in (1, 2, 3):
        send(gg, gain_x.at[x], small_ss.at[0, k], small_rs.at[0, k], xpeer(k))
        send(tg, tab_s.at[sec], small_ss.at[1, k], small_rs.at[1, k], speer(k))
    gain_x[x] = gg[...]
    tab_s[sec] = tg[...]

    remote(basis_send, basis.at[rows(z, 1 - y), :], y_ss.at[0], y_rs.at[0], partner).wait_recv()
    ring_send(1, basis, 1)

    for m in range(7):
        for direction in (0, 1):
            chunk = rs_chunk(direction, m + 1)
            remote(
                rs_recv.at[direction, m], rs_recv.at[direction, m], ring_ss.at[0, direction, m],
                ring_rs.at[0, direction, m], up if direction == 0 else down,
            ).wait_recv()
            own = g[pl.ds(2 * direction, 2), blk(chunk), :].astype(F32)
            total = (rs_recv[direction, m].astype(F32) + own).astype(BF16)
            if m < 6:
                rs_send[direction, m] = total
                rs_copy(direction, m + 1, rs_send.at[direction, m])
            else:
                zsum[pl.ds(2 * direction, 2)] = total
        ring_step(1, basis, m)

    send(zsum, ysum, y_ss.at[3], y_rs.at[3], partner)
    remote(zsum, ysum, y_ss.at[3], y_rs.at[3], partner).wait_recv()
    gx[...] = (zsum[...].astype(F32) + ysum[...].astype(F32)).astype(BF16)

    def cols(rank):
        return pl.ds(pl.multiple_of(rank * COLS, COLS), COLS)

    for k in (1, 2, 3):
        send(gx.at[lax.rem(x + k, 4)], grad.at[mine, cols(x)], x_ss.at[k], x_rs.at[k], xpeer(k))
    grad[mine, cols(x)] = gx[x]

    for k in (1, 2, 3):
        source = wrap(x - k, 4)
        remote(gg, gain_x.at[source], small_ss.at[0, k], small_rs.at[0, k], xpeer(k)).wait_recv()
        source = wrap(sec - k, 4)
        remote(tg, tab_s.at[source], small_ss.at[1, k], small_rs.at[1, k], speer(k)).wait_recv()
    gain_ys[...] = gain_x[0] + gain_x[1] + gain_x[2] + gain_x[3]
    tab_ys[...] = tab_s[0] + tab_s[1] + tab_s[2] + tab_s[3]
    send(gain_ys, gain_y, small_ss.at[0, 0], small_rs.at[0, 0], partner)
    send(tab_ys, tab_y, small_ss.at[1, 0], small_rs.at[1, 0], partner)

    for k in (1, 2, 3):
        source = wrap(x - k, 4)
        part = grad.at[mine, cols(source)]
        remote(gx.at[0], part, x_ss.at[k], x_rs.at[k], xpeer(k)).wait_recv()

    ring_send(2, grad, 0)
    ring_send(2, grad, 1)
    remote(gain_ys, gain_y, small_ss.at[0, 0], small_rs.at[0, 0], partner).wait_recv()
    remote(tab_ys, tab_y, small_ss.at[1, 0], small_rs.at[1, 0], partner).wait_recv()
    gain_z[z] = gain_ys[...] + gain_y[...]
    tab_z[z] = tab_ys[...] + tab_y[...]

    def small_ring(m, at_sender):
        origin = z if at_sender else z - 1
        slot = wrap(origin - m, NZ)
        first = (gain_z.at[slot], gain_z.at[slot], sring_ss.at[0, m], sring_rs.at[0, m], up)
        second = (tab_z.at[slot], tab_z.at[slot], sring_ss.at[1, m], sring_rs.at[1, m], up)
        return first, second

    for m in range(7):
        ring_step(2, grad, m)

    remote(ls, stat_recv, y_ss.at[2], y_rs.at[2], partner).wait_recv()

    @pl.when(y == 0)
    def _():
        prod = dot_nt(grad[mine, :], grad[...])
        top = beta_stat * ls[...] + prod[:ROWS]
        o_left[...] = top
        next_half[:ROWS] = top.astype(BF16)
        next_half[ROWS:] = (beta_stat * stat_recv[...] + prod[ROWS:]).astype(BF16)

    @pl.when(y == 1)
    def _():
        prod = dot_tn(grad[:, mine], grad[...])
        bottom = beta_stat * rs[...] + prod[ROWS:]
        o_right[...] = bottom
        next_half[:ROWS] = (beta_stat * stat_recv[...] + prod[:ROWS]).astype(BF16)
        next_half[ROWS:] = bottom.astype(BF16)

    xhalf[mine, :] = dot_nn(next_half[...], basis[...]).astype(BF16)
    ring_send(3, xhalf, 0)
    ring_send(3, xhalf, 1)

    s_copy = remote(s_buf, s_buf, y_ss.at[4], y_rs.at[4], partner)
    rot_copy = remote(rot_send, rot, y_ss.at[5], y_rs.at[5], partner)
    d_copy = remote(
        d128.at[pl.ds(0, ROWS), :], d128.at[pl.ds(0, ROWS), :], y_ss.at[6], y_rs.at[6], partner
    )
    e_copy = remote(e_send, ehalf.at[mine, :], y_ss.at[7], y_rs.at[7], partner)

    for spec in small_ring(0, True):
        send(*spec)

    def small_step(m):
        for spec in small_ring(m, False):
            remote(*spec).wait_recv()
        if m < 6:
            for spec in small_ring(m + 1, True):
                send(*spec)

    @pl.when(y == 0)
    def _():
        s_buf[...] = dot_tn(basis[:, mine], grad[...]).astype(BF16)
        s_copy.start()
        prod = dot_tn(grad[:, mine], grad[...])
        o_right[...] = beta_stat * rs[...] + prod[:ROWS]

    @pl.when(y == 1)
    def _():
        prod = dot_nt(grad[rows(z, 1), :], grad[...])
        o_left[...] = beta_stat * ls[...] + prod

    ring_step(3, xhalf, 0)
    small_step(0)
    ring_step(3, xhalf, 1)
    small_step(1)

    @pl.when(y == 1)
    def _():
        s_copy.wait_recv()
        rotated = dot_nn(s_buf[...], basis[...])
        rot_send[...] = rotated[:ROWS]
        rot_copy.start()
        rot[...] = rotated[ROWS:]

    ring_step(3, xhalf, 2)
    small_step(2)

    @pl.when(y == 0)
    def _():
        rot_copy.wait_recv()

    rotated = rot[...]
    first_new = beta_first * m1[...] + (1.0 - beta_first) * rotated
    second_new = beta_second * m2[...] + (1.0 - beta_second) * rotated * rotated
    o_first[...] = first_new
    o_second[...] = second_new
    d128[own_sub, :] = adam_direction(first_new, second_new).astype(BF16)

    @pl.when(y == 0)
    def _():
        d_copy.start()

    ring_step(3, xhalf, 3)
    small_step(3)
    ring_step(3, xhalf, 4)
    small_step(4)

    @pl.when(y == 1)
    def _():
        d_copy.wait_recv()
        e_send[...] = dot_nt(d128[...], basis[pl.ds(0, HALF), :]).astype(BF16)
        e_copy.start()
        ehalf[mine, :] = dot_nt(d128[...], basis[pl.ds(HALF, HALF), :]).astype(BF16)

    ring_step(3, xhalf, 5)
    small_step(5)

    @pl.when(y == 0)
    def _():
        e_copy.wait_recv()

    ring_send(4, ehalf, 0)
    ring_send(4, ehalf, 1)
    ring_step(3, xhalf, 6)
    small_step(6)

    def tile(i):
        return pl.ds(pl.multiple_of(i * TILE, TILE), TILE)

    def squares(i, acc):
        part = xhalf[tile(i), :].astype(F32)
        return acc + jnp.sum((part * part).reshape(TILE // 8, 8, D), axis=0)

    partial = lax.fori_loop(0, D // TILE, squares, jnp.zeros((8, D), F32))
    scale = 1.0 / jnp.sqrt(jnp.sum(partial, keepdims=True) + norm_eps)

    @pl.loop(0, D // TILE)
    def _(i):
        value = xhalf[tile(i), :].astype(F32) * scale
        xf[tile(i), :] = value
        xa[tile(i), :] = value.astype(BF16)

    def gram_pass(source):
        @pl.loop(0, D // TILE)
        def _(i):
            gram[tile(i), :] = dot_nt(source[tile(i), :], source[...]).astype(BF16)

    def apply_pass(source, target):
        @pl.loop(0, D // TILE)
        def _(i):
            value = 1.5 * xf[tile(i), :] - 0.5 * dot_nn(gram[tile(i), :], source[...])
            xf[tile(i), :] = value
            target[tile(i), :] = value.astype(BF16)

    ring_step(4, ehalf, 0)
    gram_pass(xa)
    ring_step(4, ehalf, 1)
    ring_step(4, ehalf, 2)
    apply_pass(xa, xb)
    ring_step(4, ehalf, 3)
    ring_step(4, ehalf, 4)
    gram_pass(xb)
    ring_step(4, ehalf, 5)
    apply_pass(xb, xa)
    ring_step(4, ehalf, 6)

    gram_own = dot_nt(xa[mine, :], xa[...]).astype(BF16)
    final = 1.5 * xf[mine, :] - 0.5 * dot_nn(gram_own, xa[...])

    @pl.when(y == 0)
    def _():
        o_lrot[...] = final[:ROWS]
        fin_send[...] = final[ROWS:].astype(BF16)

    @pl.when(y == 1)
    def _():
        o_rrot[...] = final[ROWS:]
        fin_send[...] = final[:ROWS].astype(BF16)

    send(fin_send, fin_recv, y_ss.at[8], y_rs.at[8], partner)

    remote(
        left128.at[own_sub, :], left128.at[pl.ds(pl.multiple_of((1 - y) * ROWS, ROWS), ROWS), :],
        y_ss.at[1], y_rs.at[1], partner,
    ).wait_recv()

    @pl.when(y == 0)
    def _():
        upd = dot_nn(left128[...], ehalf[...])
        o_update[:, :HALF] = upd[:ROWS]
        upd_send[...] = upd[ROWS:]

    @pl.when(y == 1)
    def _():
        upd = dot_nn(left128[...], ehalf[...])
        o_update[:, HALF:] = upd[ROWS:]
        upd_send[...] = upd[:ROWS]

    send(upd_send, upd_recv, y_ss.at[9], y_rs.at[9], partner)

    def total_of(slots):
        total = slots[0]
        for k in range(1, NZ):
            total = total + slots[k]
        return total

    gain_sum = total_of(gain_z)
    gain_moment = beta_first * gf[...] + (1.0 - beta_first) * gain_sum
    gain_squares = beta_second * gs[...] + (1.0 - beta_second) * gain_sum * gain_sum
    o_gm[...] = gain_moment
    o_gs[...] = gain_squares
    o_gu[...] = adam_direction(gain_moment, gain_squares)
    table_sum = total_of(tab_z)
    table_moment = beta_first * tf[...] + (1.0 - beta_first) * table_sum
    table_squares = beta_second * ts[...] + (1.0 - beta_second) * table_sum * table_sum
    o_tm[...] = table_moment
    o_ts[...] = table_squares
    o_tu[...] = adam_direction(table_moment, table_squares)

    remote(fin_send, fin_recv, y_ss.at[8], y_rs.at[8], partner).wait_recv()
    remote(upd_send, upd_recv, y_ss.at[9], y_rs.at[9], partner).wait_recv()

    @pl.when(y == 0)
    def _():
        o_rrot[...] = fin_recv[...].astype(F32)
        o_update[:, HALF:] = upd_recv[...]
        s_copy.wait_send()
        d_copy.wait_send()

    @pl.when(y == 1)
    def _():
        o_lrot[...] = fin_recv[...].astype(F32)
        o_update[:, :HALF] = upd_recv[...]
        rot_copy.wait_send()
        e_copy.wait_send()

    for copy in pending:
        copy.wait_send()


def local(
    grad_parts, first_moment, second_moment, left_stat, right_stat, left_basis, right_basis,
    gain_grads, gain_first, gain_second, table_grads, table_first, table_second,
):
    wide = jax.ShapeDtypeStruct((ROWS, D), F32)
    gain = jax.ShapeDtypeStruct((2, D), F32)
    table = jax.ShapeDtypeStruct((32, 4), F32)
    vmem = pl.BlockSpec(memory_space=pltpu.VMEM)
    dma = pltpu.SemaphoreType.DMA
    outs = pl.pallas_call(
        kernel,
        out_shape=[wide] * 7 + [gain] * 3 + [table] * 3,
        in_specs=[vmem] * 13,
        out_specs=[vmem] * 13,
        scratch_shapes=[
            pltpu.VMEM((BLK, D), BF16),
            pltpu.VMEM((ROWS, D), BF16),
            pltpu.VMEM((D, D), BF16),
            pltpu.VMEM((D, D), BF16),
            pltpu.VMEM((D, D), BF16),
            pltpu.VMEM((D, D), BF16),
            pltpu.VMEM((D, D), BF16),
            pltpu.VMEM((D, D), BF16),
            pltpu.VMEM((D, D), F32),
            pltpu.VMEM((D, HALF), BF16),
            pltpu.VMEM((2, 7, 2, BLK, COLS), BF16),
            pltpu.VMEM((2, 6, 2, BLK, COLS), BF16),
            pltpu.VMEM((4, BLK, COLS), BF16),
            pltpu.VMEM((4, BLK, COLS), BF16),
            pltpu.VMEM((4, BLK, COLS), BF16),
            pltpu.VMEM((ROWS, D), F32),
            pltpu.VMEM((BLK, D), BF16),
            pltpu.VMEM((BLK, D), BF16),
            pltpu.VMEM((ROWS, D), F32),
            pltpu.VMEM((ROWS, D), F32),
            pltpu.VMEM((BLK, D), BF16),
            pltpu.VMEM((BLK, HALF), BF16),
            pltpu.VMEM((ROWS, HALF), F32),
            pltpu.VMEM((ROWS, HALF), F32),
            pltpu.VMEM((ROWS, D), BF16),
            pltpu.VMEM((ROWS, D), BF16),
            pltpu.VMEM((4, 2, D), F32),
            pltpu.VMEM((2, D), F32),
            pltpu.VMEM((2, D), F32),
            pltpu.VMEM((NZ, 2, D), F32),
            pltpu.VMEM((4, 32, 4), F32),
            pltpu.VMEM((32, 4), F32),
            pltpu.VMEM((32, 4), F32),
            pltpu.VMEM((NZ, 32, 4), F32),
            dma((5, 2, 7)),
            dma((5, 2, 7)),
            dma((10,)),
            dma((10,)),
            dma((4,)),
            dma((4,)),
            dma((2, 4)),
            dma((2, 4)),
            dma((2, 7)),
            dma((2, 7)),
        ],
        compiler_params=pltpu.CompilerParams(
            collective_id=0, has_side_effects=True, vmem_limit_bytes=56 * 1024 * 1024
        ),
    )(
        grad_parts[0, 0], first_moment[0, 0], second_moment[0, 0], left_stat[0, 0],
        right_stat[0, 0], left_basis[0, 0], right_basis[0, 0], gain_grads[0, 0, 0],
        gain_first[0], gain_second[0], table_grads[0, 0], table_first, table_second,
    )
    return tuple(
        [value[None, None] for value in outs[:7]] + [value[None] for value in outs[7:10]]
        + list(outs[10:])
    )


def solution(mesh):
    return jax.shard_map(
        local,
        mesh=mesh,
        in_specs=(
            P("section", "dp", None, None, "tensor"),
            P("section", "tensor", "dp", None),
            P("section", "tensor", "dp", None),
            P("section", "tensor", "dp", None),
            P("section", "tensor", "dp", None),
            P("section", "tensor", "dp", None),
            P("section", "tensor", "dp", None),
            P("section", "dp", "tensor", None, None),
            P("section", None, None),
            P("section", None, None),
            P("section", "dp", None, "tensor"),
            P(None, "tensor"),
            P(None, "tensor"),
        ),
        out_specs=(
            P("section", "tensor", "dp", None),
            P("section", "tensor", "dp", None),
            P("section", "tensor", "dp", None),
            P("section", "tensor", "dp", None),
            P("section", "tensor", "dp", None),
            P("section", "tensor", "dp", None),
            P("section", "tensor", "dp", None),
            P("section", None, None),
            P("section", None, None),
            P("section", None, None),
            P(None, "tensor"),
            P(None, "tensor"),
            P(None, "tensor"),
        ),
        check_vma=False,
    )
```

time: 1100 us -> 166 us (0.15)
  waiting for transfers between devices: 666 us -> 0 us
  blocking collectives: 346 us -> 0 us
  Pallas kernels: 0 us -> 143 us
  matrix products: 32.5 us -> 0 us
  between operations: 14.7 us -> 0.71 us
  local copies, waits for them, and re-layouts: 31.6 us -> 18.9 us
    all_gather x7 -> x0, waiting for transfers between devices: 394 us -> none  [the longest x3 184 us: local(): iterate_full = lax.all_gather(iterate_half, 'dp', axis=1, tiled=True)]
    psum x3 -> x0, blocking collectives: 316 us -> none  [the longest x1 156 us: local(): gain_sum = lax.psum(gain_grads[0, 0, 0], ('dp', 'tensor'))]
    unnamed x11 -> x0, waiting for transfers between devices: 272 us -> none
    pallas_call x0 -> x1, Pallas kernels: none -> 143 us  [local(): pl.pallas_call(kernel, out_shape=[wide] * 7 + [gain] * 3 + [table] * 3, i...]
    dot_general x9 -> x0, matrix products: 32.5 us -> none  [batched(): return jnp.einsum(pattern, left, right, preferred_element_type=jnp.float32)]
    all_to_all x1 -> x0, blocking collectives: 29.7 us -> none  [local(): lax.all_to_all(partial_value, 'tensor', split_axis=0, concat_axis=2, tile...]
    transpose x1 -> x0, local copies, waits for them, and re-layouts: 11 us -> none  [batched(): return jnp.einsum(pattern, left, right, preferred_element_type=jnp.float32)]
  transfers between devices with their start and end apart: 9 -> 0, of which waited for: 7 -> 0; matrix products, arithmetic and copies ran while one was open for 4% -> 0% of each run, Pallas kernels for 0% -> 0%
where the time goes in v1:
time: 166 us; the launch traced here: 163 us
  Pallas kernels  143 us (86%)
  local copies, waits for them, and re-layouts  18.9 us (11%)
    pallas_call x1, Pallas kernels, local(): pl.pallas_call(kernel, out_shape=[wide] * 7 + [gain] * 3 + [table] * 3, i...  143 us
    unnamed x27, local copies, waits for them, and re-layouts  17.5 us

profile of v1, /device:TPU:2, one launch (start us, length us, event | category | flops | bytes accessed | tf_op | source)
XLA Modules:
  0.0 162.9 jit_solution(16496860122066710981)
XLA Ops:
  0.6 1.4 copy.26.tg
  2.0 1.4 copy.27.tf
  3.4 1.4 copy.28.ts
  4.7 143.3 %shard_map.228 = (f32[64,1024]{1,0:T(8,128)}, f32[64,1024]{1,0:T(8,128)}, f32[64,1024]{1,0:T(8,128)}, f32[64,1024]{1,0:T(8,128)}, f32[64,1024]{1,0:T(8,128)}, /*...) custom-call(bf16[4,1024,256]{2,1,0:T(8,128)(2,1)} %bitcast.21, ...), custom_call_target="tpu_custom_call" | custom-call | tf_op jit(solution)/shard_map/pallas_call | solution.py:471
  148.1 0.0 copy-start.2
  148.1 0.0 copy-start.1
  148.1 0.0 copy-start
  148.1 0.0 copy-start.5
  148.1 0.0 copy-start.4
  148.1 0.0 copy-start.3
  148.1 1.4 copy.29
  149.6 1.4 copy.30
  150.9 1.4 copy.31
  152.3 1.7 %copy.42 = f32[1,1,64,1024]{3,2,1,0:T(8,128)} copy(f32[1,1,64,1024]{3,2,1,0:T(8,128)} %bitcast.34) | data formatting | bytes 524288
  154.0 1.7 %copy.43 = f32[1,1,64,1024]{3,2,1,0:T(8,128)} copy(f32[1,1,64,1024]{3,2,1,0:T(8,128)} %bitcast.33) | data formatting | bytes 524288
  155.6 1.7 %copy.44 = f32[1,1,64,1024]{3,2,1,0:T(8,128)} copy(f32[1,1,64,1024]{3,2,1,0:T(8,128)} %bitcast.32) | data formatting | bytes 524288
  157.3 1.7 %copy.45 = f32[1,1,64,1024]{3,2,1,0:T(8,128)} copy(f32[1,1,64,1024]{3,2,1,0:T(8,128)} %bitcast.31) | data formatting | bytes 524288
  159.0 0.7 copy.46
  159.7 0.7 copy.47
  160.4 0.7 copy.48
  161.1 0.6 copy.49
  161.7 0.6 copy.50
  162.3 0.0 copy-done.3
  162.3 0.6 copy.51
  (5 shorter events, 0.0 us)
Async XLA Ops:
  148.1 10.9 %copy-start.2 = (f32[64,1024]{1,0:T(8,128)S(1)}, f32[64,1024]{1,0:T(8,128)}, u32[]{:S(2)}) copy-start(f32[64,1024]{1,0:T(8,128)} %get-tuple-element.30) | copy-start | bytes 786436
  148.1 11.6 %copy-start.1 = (f32[64,1024]{1,0:T(8,128)S(1)}, f32[64,1024]{1,0:T(8,128)}, u32[]{:S(2)}) copy-start(f32[64,1024]{1,0:T(8,128)} %get-tuple-element.31) | copy-start | bytes 786436
  148.1 12.3 %copy-start = (f32[64,1024]{1,0:T(8,128)S(1)}, f32[64,1024]{1,0:T(8,128)}, u32[]{:S(2)}) copy-start(f32[64,1024]{1,0:T(8,128)} %get-tuple-element.32) | copy-start | bytes 786436
  148.1 13.0 %copy-start.5 = (f32[2,1024]{1,0:T(2,128)S(1)}, f32[2,1024]{1,0:T(2,128)}, u32[]{:S(2)}) copy-start(f32[2,1024]{1,0:T(2,128)} %get-tuple-element.33) | copy-start | bytes 24580
  148.1 13.6 %copy-start.4 = (f32[2,1024]{1,0:T(2,128)S(1)}, f32[2,1024]{1,0:T(2,128)}, u32[]{:S(2)}) copy-start(f32[2,1024]{1,0:T(2,128)} %get-tuple-element.34) | copy-start | bytes 24580
  148.1 14.2 %copy-start.3 = (f32[2,1024]{1,0:T(2,128)S(1)}, f32[2,1024]{1,0:T(2,128)}, u32[]{:S(2)}) copy-start(f32[2,1024]{1,0:T(2,128)} %get-tuple-element.35) | copy-start | bytes 24580

commit v2 on v1

--- a/solution.py
+++ b/solution.py
@@ -47,15 +47,33 @@
 
 
 def kernel(
-    g, m1, m2, ls, rs, lb, rb, gg, gf, gs, tg, tf, ts,
+    g_hbm, m1_hbm, m2_hbm, ls_hbm, rs_hbm, lb_hbm, rb_hbm, gg, gf, gs, tg, tf, ts,
     o_update, o_first, o_second, o_left, o_right, o_lrot, o_rrot,
     o_gu, o_gm, o_gs, o_tu, o_tm, o_ts,
+    g, m1, m2, ls, rs, lb, rb,
+    v_update, v_first, v_second, v_left, v_right, v_lrot, v_rrot,
     left128, basis_send, basis, grad, xhalf, xa, xb, gram, xf, ehalf,
     rs_recv, rs_send, zsum, ysum, gx, stat_recv, next_half,
-    s_buf, rot, rot_send, d128, e_send, upd_send, upd_recv, fin_send, fin_recv,
+    s_buf, rot, rot_send, rot_recv, d128, e_send, upd_send, upd_recv, fin_send, fin_recv,
     gain_x, gain_y, gain_ys, gain_z, tab_s, tab_y, tab_ys, tab_z,
+    in_sem, out_sem, red_ss, red_rs,
     ring_ss, ring_rs, y_ss, y_rs, x_ss, x_rs, small_ss, small_rs, sring_ss, sring_rs,
 ):
+    sources = [lb_hbm, rb_hbm, g_hbm, ls_hbm, rs_hbm, m1_hbm, m2_hbm]
+    targets = [lb, rb, g, ls, rs, m1, m2]
+    loads = [
+        pltpu.make_async_copy(source, target, in_sem.at[i])
+        for i, (source, target) in enumerate(zip(sources, targets))
+    ]
+    for load in loads:
+        load.start()
+    stores = []
+
+    def emit(source, target):
+        copy = pltpu.make_async_copy(source, target, out_sem.at[len(stores)])
+        copy.start()
+        stores.append(copy)
+
     dp = lax.axis_index("dp")
     x = lax.axis_index("tensor")
     sec = lax.axis_index("section")
@@ -97,6 +115,7 @@
 
     mine = blk(z)
     own_sub = pl.ds(pl.multiple_of(y * ROWS, ROWS), ROWS)
+    other_sub = pl.ds(pl.multiple_of((1 - y) * ROWS, ROWS), ROWS)
 
     def ring_spec(phase, buf, direction, m, at_sender):
         step = m // 2
@@ -115,31 +134,30 @@
         for direction in (0, 1):
             send(*ring_spec(phase, buf, direction, m, True))
 
-    def ring_wait(phase, buf, m):
+    def ring_step(phase, buf, m):
         for direction in (0, 1):
             remote(*ring_spec(phase, buf, direction, m, False)).wait_recv()
-
-    def ring_step(phase, buf, m):
-        ring_wait(phase, buf, m)
-        if m < 4:
-            ring_send(phase, buf, m + 2)
-        elif m == 4:
-            send(*ring_spec(phase, buf, 0, 6, True))
-        elif m == 5:
-            send(*ring_spec(phase, buf, 1, 6, True))
+            if m < 4:
+                send(*ring_spec(phase, buf, direction, m + 2, True))
+            elif m == 4 + direction:
+                send(*ring_spec(phase, buf, direction, 6, True))
 
     def rs_chunk(direction, step):
         return wrap(z - 1 - step if direction == 0 else z + 1 + step, NZ)
 
-    def rs_copy(direction, step, src):
-        send(
-            src, rs_recv.at[direction, step], ring_ss.at[0, direction, step],
-            ring_rs.at[0, direction, step], up if direction == 0 else down,
+    def rs_copy(direction, chain, step, src):
+        return (
+            src, rs_recv.at[direction, step, chain], red_ss.at[direction, chain, step],
+            red_rs.at[direction, chain, step], up if direction == 0 else down,
         )
 
-    for direction in (0, 1):
-        rs_copy(direction, 0, g.at[pl.ds(2 * direction, 2), blk(rs_chunk(direction, 0)), :])
-
+    for chain in (0, 1):
+        for direction in (0, 1):
+            first = g_hbm.at[2 * direction + chain, blk(rs_chunk(direction, 0)), :]
+            send(*rs_copy(direction, chain, 0, first))
+
+    loads[0].wait()
+    loads[1].wait()
     lhalf = lb[...].astype(BF16)
     rhalf = rb[...].astype(BF16)
     left128[own_sub, :] = lhalf
@@ -156,20 +174,6 @@
 
     send(basis_send, basis.at[rows(z, y), :], y_ss.at[0], y_rs.at[0], partner)
     ring_send(1, basis, 0)
-    send(left128.at[own_sub, :], left128.at[own_sub, :], y_ss.at[1], y_rs.at[1], partner)
-
-    def stat_copy(src):
-        return remote(src, stat_recv, y_ss.at[2], y_rs.at[2], partner)
-
-    @pl.when(y == 0)
-    def _():
-        stat_copy(rs).start()
-
-    @pl.when(y == 1)
-    def _():
-        stat_copy(ls).start()
-
-    pending.append(stat_copy(ls))
 
     for k in (1, 2, 3):
         send(gg, gain_x.at[x], small_ss.at[0, k], small_rs.at[0, k], xpeer(k))
@@ -177,35 +181,70 @@
     gain_x[x] = gg[...]
     tab_s[sec] = tg[...]
 
+    def stat_copy(src):
+        return remote(src, stat_recv, y_ss.at[2], y_rs.at[2], partner)
+
+    @pl.when(y == 0)
+    def _():
+        stat_copy(rs_hbm).start()
+
+    @pl.when(y == 1)
+    def _():
+        stat_copy(ls_hbm).start()
+
+    pending.append(stat_copy(ls_hbm))
+    send(left128.at[own_sub, :], left128.at[own_sub, :], y_ss.at[1], y_rs.at[1], partner)
     remote(basis_send, basis.at[rows(z, 1 - y), :], y_ss.at[0], y_rs.at[0], partner).wait_recv()
     ring_send(1, basis, 1)
+    loads[2].wait()
+
+    def swap_spec(mat):
+        return (zsum.at[mat], ysum.at[mat], y_ss.at[10 + mat], y_rs.at[10 + mat], partner)
 
     for m in range(7):
-        for direction in (0, 1):
-            chunk = rs_chunk(direction, m + 1)
-            remote(
-                rs_recv.at[direction, m], rs_recv.at[direction, m], ring_ss.at[0, direction, m],
-                ring_rs.at[0, direction, m], up if direction == 0 else down,
-            ).wait_recv()
-            own = g[pl.ds(2 * direction, 2), blk(chunk), :].astype(F32)
-            total = (rs_recv[direction, m].astype(F32) + own).astype(BF16)
-            if m < 6:
-                rs_send[direction, m] = total
-                rs_copy(direction, m + 1, rs_send.at[direction, m])
-            else:
-                zsum[pl.ds(2 * direction, 2)] = total
-        ring_step(1, basis, m)
-
-    send(zsum, ysum, y_ss.at[3], y_rs.at[3], partner)
-    remote(zsum, ysum, y_ss.at[3], y_rs.at[3], partner).wait_recv()
-    gx[...] = (zsum[...].astype(F32) + ysum[...].astype(F32)).astype(BF16)
+        for chain in (0, 1):
+            for direction in (0, 1):
+                mat = 2 * direction + chain
+                landed = rs_recv.at[direction, m, chain]
+                remote(*rs_copy(direction, chain, m, landed)).wait_recv()
+                own = g[mat, blk(rs_chunk(direction, m + 1)), :].astype(F32)
+                total = (landed[...].astype(F32) + own).astype(BF16)
+                if m < 6:
+                    rs_send[direction, m, chain] = total
+                    send(*rs_copy(direction, chain, m + 1, rs_send.at[direction, m, chain]))
+                else:
+                    zsum[mat] = total
+                    send(*swap_spec(mat))
+        if m in (2, 4):
+            ring_step(1, basis, m // 2 - 1)
+    ring_step(1, basis, 2)
 
     def cols(rank):
         return pl.ds(pl.multiple_of(rank * COLS, COLS), COLS)
 
+    for chain in (0, 1):
+        for direction in (0, 1):
+            mat = 2 * direction + chain
+            remote(*swap_spec(mat)).wait_recv()
+            gx[mat] = (zsum[mat].astype(F32) + ysum[mat].astype(F32)).astype(BF16)
+
+            @pl.when(x == mat)
+            def _(mat=mat):
+                grad[mine, cols(x)] = gx[mat]
+
+            @pl.when(x != mat)
+            def _(mat=mat):
+                k = wrap(mat - x, 4)
+                remote(
+                    gx.at[mat], grad.at[mine, cols(x)], x_ss.at[k], x_rs.at[k], {"tensor": mat}
+                ).start()
+
     for k in (1, 2, 3):
-        send(gx.at[lax.rem(x + k, 4)], grad.at[mine, cols(x)], x_ss.at[k], x_rs.at[k], xpeer(k))
-    grad[mine, cols(x)] = gx[x]
+        pending.append(
+            remote(gx.at[0], grad.at[mine, cols(x)], x_ss.at[k], x_rs.at[k], xpeer(k))
+        )
+    ring_step(1, basis, 3)
+    ring_step(1, basis, 4)
 
     for k in (1, 2, 3):
         source = wrap(x - k, 4)
@@ -218,12 +257,12 @@
     send(tab_ys, tab_y, small_ss.at[1, 0], small_rs.at[1, 0], partner)
 
     for k in (1, 2, 3):
-        source = wrap(x - k, 4)
-        part = grad.at[mine, cols(source)]
+        part = grad.at[mine, cols(wrap(x - k, 4))]
         remote(gx.at[0], part, x_ss.at[k], x_rs.at[k], xpeer(k)).wait_recv()
 
     ring_send(2, grad, 0)
     ring_send(2, grad, 1)
+    ring_step(1, basis, 5)
     remote(gain_ys, gain_y, small_ss.at[0, 0], small_rs.at[0, 0], partner).wait_recv()
     remote(tab_ys, tab_y, small_ss.at[1, 0], small_rs.at[1, 0], partner).wait_recv()
     gain_z[z] = gain_ys[...] + gain_y[...]
@@ -238,14 +277,18 @@
 
     for m in range(7):
         ring_step(2, grad, m)
-
-    remote(ls, stat_recv, y_ss.at[2], y_rs.at[2], partner).wait_recv()
+        if m == 2:
+            ring_step(1, basis, 6)
+
+    remote(ls_hbm, stat_recv, y_ss.at[2], y_rs.at[2], partner).wait_recv()
+    for load in loads[3:]:
+        load.wait()
 
     @pl.when(y == 0)
     def _():
         prod = dot_nt(grad[mine, :], grad[...])
         top = beta_stat * ls[...] + prod[:ROWS]
-        o_left[...] = top
+        v_left[...] = top
         next_half[:ROWS] = top.astype(BF16)
         next_half[ROWS:] = (beta_stat * stat_recv[...] + prod[ROWS:]).astype(BF16)
 
@@ -253,7 +296,7 @@
     def _():
         prod = dot_tn(grad[:, mine], grad[...])
         bottom = beta_stat * rs[...] + prod[ROWS:]
-        o_right[...] = bottom
+        v_right[...] = bottom
         next_half[:ROWS] = (beta_stat * stat_recv[...] + prod[:ROWS]).astype(BF16)
         next_half[ROWS:] = bottom.astype(BF16)
 
@@ -262,7 +305,7 @@
     ring_send(3, xhalf, 1)
 
     s_copy = remote(s_buf, s_buf, y_ss.at[4], y_rs.at[4], partner)
-    rot_copy = remote(rot_send, rot, y_ss.at[5], y_rs.at[5], partner)
+    rot_copy = remote(rot_send, rot_recv, y_ss.at[5], y_rs.at[5], partner)
     d_copy = remote(
         d128.at[pl.ds(0, ROWS), :], d128.at[pl.ds(0, ROWS), :], y_ss.at[6], y_rs.at[6], partner
     )
@@ -283,48 +326,56 @@
         s_buf[...] = dot_tn(basis[:, mine], grad[...]).astype(BF16)
         s_copy.start()
         prod = dot_tn(grad[:, mine], grad[...])
-        o_right[...] = beta_stat * rs[...] + prod[:ROWS]
+        v_right[...] = beta_stat * rs[...] + prod[:ROWS]
 
     @pl.when(y == 1)
     def _():
         prod = dot_nt(grad[rows(z, 1), :], grad[...])
-        o_left[...] = beta_stat * ls[...] + prod
-
+        v_left[...] = beta_stat * ls[...] + prod
+
+    emit(v_left, o_left)
+    emit(v_right, o_right)
     ring_step(3, xhalf, 0)
     small_step(0)
     ring_step(3, xhalf, 1)
     small_step(1)
+    ring_step(3, xhalf, 2)
 
     @pl.when(y == 1)
     def _():
         s_copy.wait_recv()
         rotated = dot_nn(s_buf[...], basis[...])
-        rot_send[...] = rotated[:ROWS]
+        rot_send[...] = rotated[:ROWS].astype(BF16)
         rot_copy.start()
         rot[...] = rotated[ROWS:]
 
-    ring_step(3, xhalf, 2)
     small_step(2)
+    ring_step(3, xhalf, 3)
+    small_step(3)
+    ring_step(3, xhalf, 4)
 
     @pl.when(y == 0)
     def _():
         rot_copy.wait_recv()
+        rot[...] = rot_recv[...].astype(F32)
 
     rotated = rot[...]
     first_new = beta_first * m1[...] + (1.0 - beta_first) * rotated
     second_new = beta_second * m2[...] + (1.0 - beta_second) * rotated * rotated
-    o_first[...] = first_new
-    o_second[...] = second_new
+    v_first[...] = first_new
+    v_second[...] = second_new
     d128[own_sub, :] = adam_direction(first_new, second_new).astype(BF16)
 
     @pl.when(y == 0)
     def _():
         d_copy.start()
 
-    ring_step(3, xhalf, 3)
-    small_step(3)
-    ring_step(3, xhalf, 4)
+    emit(v_first, o_first)
+    emit(v_second, o_second)
     small_step(4)
+    ring_step(3, xhalf, 5)
+    small_step(5)
+    ring_step(3, xhalf, 6)
 
     @pl.when(y == 1)
     def _():
@@ -332,18 +383,6 @@
         e_send[...] = dot_nt(d128[...], basis[pl.ds(0, HALF), :]).astype(BF16)
         e_copy.start()
         ehalf[mine, :] = dot_nt(d128[...], basis[pl.ds(HALF, HALF), :]).astype(BF16)
-
-    ring_step(3, xhalf, 5)
-    small_step(5)
-
-    @pl.when(y == 0)
-    def _():
-        e_copy.wait_recv()
-
-    ring_send(4, ehalf, 0)
-    ring_send(4, ehalf, 1)
-    ring_step(3, xhalf, 6)
-    small_step(6)
 
     def tile(i):
         return pl.ds(pl.multiple_of(i * TILE, TILE), TILE)
@@ -361,61 +400,72 @@
         xf[tile(i), :] = value
         xa[tile(i), :] = value.astype(BF16)
 
-    def gram_pass(source):
-        @pl.loop(0, D // TILE)
+    def gram_pass(source, half):
+        @pl.loop(2 * half, 2 * half + 2)
         def _(i):
             gram[tile(i), :] = dot_nt(source[tile(i), :], source[...]).astype(BF16)
 
-    def apply_pass(source, target):
-        @pl.loop(0, D // TILE)
+    def apply_pass(source, target, half):
+        @pl.loop(2 * half, 2 * half + 2)
         def _(i):
             value = 1.5 * xf[tile(i), :] - 0.5 * dot_nn(gram[tile(i), :], source[...])
             xf[tile(i), :] = value
             target[tile(i), :] = value.astype(BF16)
 
+    gram_pass(xa, 0)
+
+    @pl.when(y == 0)
+    def _():
+        e_copy.wait_recv()
+
+    ring_send(4, ehalf, 0)
+    ring_send(4, ehalf, 1)
+    small_step(6)
+    gram_pass(xa, 1)
+    apply_pass(xa, xb, 0)
     ring_step(4, ehalf, 0)
-    gram_pass(xa)
+    apply_pass(xa, xb, 1)
     ring_step(4, ehalf, 1)
+    gram_pass(xb, 0)
     ring_step(4, ehalf, 2)
-    apply_pass(xa, xb)
+    gram_pass(xb, 1)
     ring_step(4, ehalf, 3)
+    apply_pass(xb, xa, 0)
     ring_step(4, ehalf, 4)
-    gram_pass(xb)
+    apply_pass(xb, xa, 1)
     ring_step(4, ehalf, 5)
-    apply_pass(xb, xa)
-    ring_step(4, ehalf, 6)
 
     gram_own = dot_nt(xa[mine, :], xa[...]).astype(BF16)
     final = 1.5 * xf[mine, :] - 0.5 * dot_nn(gram_own, xa[...])
 
     @pl.when(y == 0)
     def _():
-        o_lrot[...] = final[:ROWS]
+        v_lrot[...] = final[:ROWS]
         fin_send[...] = final[ROWS:].astype(BF16)
 
     @pl.when(y == 1)
     def _():
-        o_rrot[...] = final[ROWS:]
+        v_rrot[...] = final[ROWS:]
         fin_send[...] = final[:ROWS].astype(BF16)
 
     send(fin_send, fin_recv, y_ss.at[8], y_rs.at[8], partner)
+    ring_step(4, ehalf, 6)
 
     remote(
-        left128.at[own_sub, :], left128.at[pl.ds(pl.multiple_of((1 - y) * ROWS, ROWS), ROWS), :],
-        y_ss.at[1], y_rs.at[1], partner,
+        left128.at[own_sub, :], left128.at[other_sub, :], y_ss.at[1], y_rs.at[1], partner
     ).wait_recv()
 
     @pl.when(y == 0)
     def _():
         upd = dot_nn(left128[...], ehalf[...])
-        o_update[:, :HALF] = upd[:ROWS]
-        upd_send[...] = upd[ROWS:]
+        v_update[:, :HALF] = upd[:ROWS]
+        upd_send[...] = upd[ROWS:].astype(BF16)
 
     @pl.when(y == 1)
     def _():
         upd = dot_nn(left128[...], ehalf[...])
-        o_update[:, HALF:] = upd[ROWS:]
-        upd_send[...] = upd[:ROWS]
+        v_update[:, HALF:] = upd[ROWS:]
+        upd_send[...] = upd[:ROWS].astype(BF16)
 
     send(upd_send, upd_recv, y_ss.at[9], y_rs.at[9], partner)
 
@@ -439,24 +489,50 @@
     o_tu[...] = adam_direction(table_moment, table_squares)
 
     remote(fin_send, fin_recv, y_ss.at[8], y_rs.at[8], partner).wait_recv()
+
+    @pl.when(y == 0)
+    def _():
+        v_rrot[...] = fin_recv[...].astype(F32)
+
+    @pl.when(y == 1)
+    def _():
+        v_lrot[...] = fin_recv[...].astype(F32)
+
+    emit(v_lrot, o_lrot)
+    emit(v_rrot, o_rrot)
     remote(upd_send, upd_recv, y_ss.at[9], y_rs.at[9], partner).wait_recv()
 
     @pl.when(y == 0)
     def _():
-        o_rrot[...] = fin_recv[...].astype(F32)
-        o_update[:, HALF:] = upd_recv[...]
+        v_update[:, HALF:] = upd_recv[...].astype(F32)
         s_copy.wait_send()
         d_copy.wait_send()
 
     @pl.when(y == 1)
     def _():
-        o_lrot[...] = fin_recv[...].astype(F32)
-        o_update[:, :HALF] = upd_recv[...]
+        v_update[:, :HALF] = upd_recv[...].astype(F32)
         rot_copy.wait_send()
         e_copy.wait_send()
 
+    emit(v_update, o_update)
     for copy in pending:
         copy.wait_send()
+    for copy in stores:
+        copy.wait()
+
+
+def write_out(*refs):
+    n = 13
+    ins, outs, bufs, (in_sem, out_sem) = refs[:n], refs[n : 2 * n], refs[2 * n : 3 * n], refs[3 * n :]
+    loads = [pltpu.make_async_copy(ins[i], bufs[i], in_sem.at[i]) for i in range(n)]
+    stores = [pltpu.make_async_copy(bufs[i], outs[i], out_sem.at[i]) for i in range(n)]
+    for load in loads:
+        load.start()
+    for load, store in zip(loads, stores):
+        load.wait()
+        store.start()
+    for store in stores:
+        store.wait()
 
 
 def local(
@@ -465,15 +541,20 @@
 ):
     wide = jax.ShapeDtypeStruct((ROWS, D), F32)
     gain = jax.ShapeDtypeStruct((2, D), F32)
-    table = jax.ShapeDtypeStruct((32, 4), F32)
+    table = jax.ShapeDtypeStruct((4, 32), F32)
+    shapes = [wide] * 7 + [gain] * 3 + [table] * 3
     vmem = pl.BlockSpec(memory_space=pltpu.VMEM)
+    hbm = pl.BlockSpec(memory_space=pl.ANY)
     dma = pltpu.SemaphoreType.DMA
     outs = pl.pallas_call(
         kernel,
-        out_shape=[wide] * 7 + [gain] * 3 + [table] * 3,
-        in_specs=[vmem] * 13,
-        out_specs=[vmem] * 13,
+        out_shape=shapes,
+        in_specs=[hbm] * 7 + [vmem] * 6,
+        out_specs=[hbm] * 7 + [vmem] * 6,
         scratch_shapes=[
+            pltpu.VMEM((4, D, COLS), BF16),
+            *[pltpu.VMEM((ROWS, D), F32)] * 6,
+            *[pltpu.VMEM((ROWS, D), F32)] * 7,
             pltpu.VMEM((BLK, D), BF16),
             pltpu.VMEM((ROWS, D), BF16),
             pltpu.VMEM((D, D), BF16),
@@ -493,25 +574,30 @@
             pltpu.VMEM((BLK, D), BF16),
             pltpu.VMEM((BLK, D), BF16),
             pltpu.VMEM((ROWS, D), F32),
-            pltpu.VMEM((ROWS, D), F32),
+            pltpu.VMEM((ROWS, D), BF16),
+            pltpu.VMEM((ROWS, D), BF16),
             pltpu.VMEM((BLK, D), BF16),
             pltpu.VMEM((BLK, HALF), BF16),
-            pltpu.VMEM((ROWS, HALF), F32),
-            pltpu.VMEM((ROWS, HALF), F32),
+            pltpu.VMEM((ROWS, HALF), BF16),
+            pltpu.VMEM((ROWS, HALF), BF16),
             pltpu.VMEM((ROWS, D), BF16),
             pltpu.VMEM((ROWS, D), BF16),
             pltpu.VMEM((4, 2, D), F32),
             pltpu.VMEM((2, D), F32),
             pltpu.VMEM((2, D), F32),
             pltpu.VMEM((NZ, 2, D), F32),
-            pltpu.VMEM((4, 32, 4), F32),
-            pltpu.VMEM((32, 4), F32),
-            pltpu.VMEM((32, 4), F32),
-            pltpu.VMEM((NZ, 32, 4), F32),
+            pltpu.VMEM((4, 4, 32), F32),
+            pltpu.VMEM((4, 32), F32),
+            pltpu.VMEM((4, 32), F32),
+            pltpu.VMEM((NZ, 4, 32), F32),
+            dma((7,)),
+            dma((7,)),
+            dma((2, 2, 7)),
+            dma((2, 2, 7)),
             dma((5, 2, 7)),
             dma((5, 2, 7)),
-            dma((10,)),
-            dma((10,)),
+            dma((14,)),
+            dma((14,)),
             dma((4,)),
             dma((4,)),
             dma((2, 4)),
@@ -525,11 +611,18 @@
     )(
         grad_parts[0, 0], first_moment[0, 0], second_moment[0, 0], left_stat[0, 0],
         right_stat[0, 0], left_basis[0, 0], right_basis[0, 0], gain_grads[0, 0, 0],
-        gain_first[0], gain_second[0], table_grads[0, 0], table_first, table_second,
+        gain_first[0], gain_second[0], table_grads[0, 0].T, table_first.T, table_second.T,
     )
+    outs = pl.pallas_call(
+        write_out,
+        out_shape=shapes,
+        in_specs=[hbm] * 13,
+        out_specs=[hbm] * 13,
+        scratch_shapes=[*[pltpu.VMEM(s.shape, s.dtype) for s in shapes], dma((13,)), dma((13,))],
+    )(*outs)
     return tuple(
         [value[None, None] for value in outs[:7]] + [value[None] for value in outs[7:10]]
-        + list(outs[10:])
+        + [value.T for value in outs[10:]]
     )
 
 

time: 166 us -> 136 us (0.82)
  local copies, waits for them, and re-layouts: 18.9 us -> 0 us
  Pallas kernels: 143 us -> 134 us
    unnamed x27 -> x0, local copies, waits for them, and re-layouts: 17.5 us -> none
    pallas_call x1 -> x2, Pallas kernels: 143 us -> 134 us  [the longest x1 131 us: local(): pl.pallas_call(kernel, out_shape=shapes, in_specs=[hbm] * 7 + [vmem] * 6,...]
where the time goes in v2:
time: 136 us; the launch traced here: 134 us
  Pallas kernels  134 us (99%)
    pallas_call x1, Pallas kernels, local(): pl.pallas_call(kernel, out_shape=shapes, in_specs=[hbm] * 7 + [vmem] * 6,...  131 us

profile of v2, /device:TPU:2, one launch (start us, length us, event | category | flops | bytes accessed | tf_op | source)
XLA Modules:
  0.0 134.3 jit_solution(2387989412815708134)
XLA Ops:
  0.6 131.2 %shard_map.228 = (f32[64,1024]{1,0:T(8,128)}, f32[64,1024]{1,0:T(8,128)}, f32[64,1024]{1,0:T(8,128)}, f32[64,1024]{1,0:T(8,128)}, f32[64,1024]{1,0:T(8,128)}, /*...) custom-call(bf16[4,1024,256]{2,1,0:T(8,128)(2,1)} %bitcast.28, ...), custom_call_target="tpu_custom_call" | custom-call | tf_op jit(solution)/shard_map/pallas_call | solution.py:549
  131.9 2.4 %shard_map.229 = (f32[64,1024]{1,0:T(8,128)}, f32[64,1024]{1,0:T(8,128)}, f32[64,1024]{1,0:T(8,128)}, f32[64,1024]{1,0:T(8,128)}, f32[64,1024]{1,0:T(8,128)}, /*...) custom-call(f32[64,1024]{1,0:T(8,128)} %get-tuple-element.39.refs_0_, ...), custom_call_target="tpu_custom_call" | custom-call | tf_op jit(solution)/shard_map/pallas_call | solution.py:616
